TPU v7x, 512 devices: a whole 4x4x16 slice. The times are simulated.
512 devices in a mesh: grp: 16 (over y, x), ch: 32 (over z, core).
Axes of the slice: x: 4, y: 4, z: 16, core: 2. Of those that a mesh axis runs over, the one named last changes fastest.
Arguments:
- x_in: bfloat16 [65536, 8192], P(('grp', 'ch')), may hold values from -6 to 6
- bc_in: bfloat16 [65536, 256], P(('grp', 'ch')), may hold values from -6 to 6
- dt_in: bfloat16 [65536, 128], P(('grp', 'ch')), may hold values from -2 to 14
- dt_bias: float32 [128], replicated, may hold values from -3 to -1
- a_log: float32 [128], P('ch'), may hold values from -7.5 to 0
- skip_d: float32 [128], P('ch'), may hold values from 0.5 to 1.5
- conv_x: float32 [4, 8192], P(None, 'ch'), may hold values from -3 to 3
- conv_x_bias: float32 [8192], P('ch'), may hold values from -3 to 3
- conv_bc: float32 [4, 256], replicated, may hold values from -3 to 3
- conv_bc_bias: float32 [256], replicated, may hold values from -3 to 3
- norm_gain: float32 [8192], replicated, may hold values from 0.5 to 1.5
- lengths: int32 [256], replicated, may hold values from 64 to 256, as said below
- dest_group: int32 [256], replicated, may hold values from -1 to 15, as said below
- dest_slot: int32 [256], replicated, may hold values from -1 to 15, as said below
Outputs:
- mixer_out: bfloat16 [65536, 8192], P(('grp', 'ch'))
Inputs may be any that keep to these rules, and one draw needn't show every extreme that they name: `dest_group`: -1 marks a dropped pair. From one group at most 2 surviving pairs go to any one group, and every group sends exactly 2 to some group; one group's pairs go to at most 8 groups. `dest_slot`: -1 exactly where dest_group is -1; no two surviving pairs share a destination group and slot. `lengths`: every group holds at least one pair of length 256.
All inputs are finite; a program needn't handle non-finite values.
Results may differ from a plain program's by a relative error of at most 0.0053.
Values may be sent and summed in bfloat16 or wider, within the bound.
No kernel may reach another device: no remote copies, remote signals or barrier semaphores. Data moves between devices by JAX's collectives and lax.ppermute only.
A program may use at most 64 MiB of HBM per device.

v0:
```python
import jax
import jax.numpy as jnp
from jax import lax
from jax.sharding import PartitionSpec as P

CAP = 2


def conv_silu(values, taps, bias):
    tap_count = taps.shape[0]
    length = values.shape[0]
    padded = jnp.concatenate(
        [jnp.zeros((tap_count - 1, values.shape[1]), jnp.float32), values], axis=0
    )
    total = jnp.zeros_like(values) + bias[None, :]
    for offset in range(tap_count):
        total = total + taps[offset][None, :] * padded[offset : offset + length]
    return jax.nn.silu(total)


def mix_pair(
    x_pair, bc_pair, step_pair, conv_x, conv_x_bias, conv_bc, conv_bc_bias, decay_rate, skip_gain
):
    length, chan_width = x_pair.shape
    head_count = decay_rate.shape[0]
    head_dim = chan_width // head_count
    state_dim = bc_pair.shape[1] // 2
    x_conv = conv_silu(x_pair.astype(jnp.float32), conv_x, conv_x_bias)
    bc_conv = conv_silu(bc_pair.astype(jnp.float32), conv_bc, conv_bc_bias)
    b_part = bc_conv[:, :state_dim]
    c_part = bc_conv[:, state_dim:]
    step_size = step_pair.astype(jnp.float32)
    log_decay = jnp.cumsum(-step_size * decay_rate[None, :], axis=0).T
    log_ratio = log_decay[:, :, None] - log_decay[:, None, :]
    later = jnp.arange(length, dtype=jnp.int32)[:, None]
    earlier = jnp.arange(length, dtype=jnp.int32)[None, :]
    causal = later >= earlier
    decay_mask = jnp.where(causal[None], jnp.exp(jnp.minimum(log_ratio, 0.0)), 0.0)
    scores = jnp.dot(
        c_part, b_part.T, precision=lax.Precision.HIGHEST, preferred_element_type=jnp.float32
    )
    weights = scores[None] * decay_mask * step_size.T[:, None, :]
    x_heads = x_conv.reshape(length, head_count, head_dim)
    mixed_out = jnp.einsum("hts,shp->thp", weights, x_heads, precision=lax.Precision.HIGHEST)
    mixed_out = mixed_out + skip_gain[None, :, None] * x_heads
    return mixed_out.reshape(length, chan_width).astype(jnp.bfloat16)


def route_plan(dest_group, dest_slot, my_group, n_grp, pair_count):
    by_group = dest_group.reshape(n_grp, pair_count)
    group_ids = jnp.arange(n_grp, dtype=jnp.int32)
    matches = (by_group[:, :, None] == group_ids[None, None, :]).astype(jnp.int32)
    earlier = jnp.cumsum(matches, axis=1) - matches
    ranking = jnp.sum(earlier * matches, axis=2)
    own_dest = by_group[my_group]
    own_rank = ranking[my_group]
    wanted = jnp.arange(n_grp * CAP, dtype=jnp.int32)
    wanted_group = wanted // CAP
    wanted_rank = wanted % CAP
    chosen = (own_dest[None, :] == wanted_group[:, None]) & (
        own_rank[None, :] == wanted_rank[:, None]
    )
    pair_ids = jnp.arange(pair_count, dtype=jnp.int32)
    send_index = jnp.where(
        jnp.any(chosen, axis=1),
        jnp.sum(chosen.astype(jnp.int32) * pair_ids[None, :], axis=1),
        pair_count,
    )
    arrivals = (dest_group[None, :] == my_group) & (dest_slot[None, :] == pair_ids[:, None])
    filled = jnp.any(arrivals, axis=1)
    all_ids = jnp.arange(n_grp * pair_count, dtype=jnp.int32)
    sources = jnp.sum(arrivals.astype(jnp.int32) * all_ids[None, :], axis=1)
    recv_index = sources // pair_count * CAP + ranking.reshape(-1)[sources]
    return (send_index, recv_index, filled)


def per_device(
    x_in,
    bc_in,
    dt_in,
    dt_bias,
    a_log,
    skip_d,
    conv_x,
    conv_x_bias,
    conv_bc,
    conv_bc_bias,
    norm_gain,
    lengths,
    dest_group,
    dest_slot,
):
    n_ch = lax.axis_size("ch")
    n_grp = lax.axis_size("grp")
    my_chan = lax.axis_index("ch")
    my_group = lax.axis_index("grp")
    tok_rows = x_in.shape[0]
    pair_len = 2 * tok_rows
    pair_count = n_ch * tok_rows // pair_len
    first_token = my_chan * tok_rows
    own_pair = my_group * pair_count + first_token // pair_len
    positions = first_token % pair_len + jnp.arange(tok_rows, dtype=jnp.int32)
    valid = positions < lengths[own_pair]
    x_masked = jnp.where(valid[:, None], x_in, jnp.zeros_like(x_in))
    bc_masked = jnp.where(valid[:, None], bc_in, jnp.zeros_like(bc_in))
    step_rows = (
        jax.nn.softplus(dt_in.astype(jnp.float32) + dt_bias[None, :])
        * valid[:, None].astype(jnp.float32)
    ).astype(jnp.bfloat16)
    x_chan, bc_cols, dt_chan = (
        lax.all_to_all(x_masked, "ch", split_axis=1, concat_axis=0, tiled=True),
        lax.all_to_all(bc_masked, "ch", split_axis=1, concat_axis=0, tiled=True),
        lax.all_to_all(step_rows, "ch", split_axis=1, concat_axis=0, tiled=True),
    )
    chan_width = x_chan.shape[1]
    head_local = dt_chan.shape[1]
    x_pairs = x_chan.reshape(pair_count, pair_len, chan_width)
    dt_pairs = dt_chan.reshape(pair_count, pair_len * head_local)
    decay_rate = jnp.exp(a_log)
    send_index, recv_index, filled = route_plan(dest_group, dest_slot, my_group, n_grp, pair_count)

    def outgoing(blocks):
        picked = jnp.take(blocks, send_index, axis=0, mode="fill", fill_value=0)
        return picked.reshape((n_grp, CAP) + blocks.shape[1:])

    def incoming(arrived):
        flat = arrived.reshape((n_grp * CAP,) + arrived.shape[2:])
        return jnp.take(flat, recv_index, axis=0)

    bc_col_pairs = bc_cols.reshape(pair_count, pair_len, bc_cols.shape[1])
    x_recv, bc_recv, dt_recv = (
        lax.all_to_all(outgoing(x_pairs), "grp", split_axis=0, concat_axis=0, tiled=True),
        lax.all_to_all(outgoing(bc_col_pairs), "grp", split_axis=0, concat_axis=0, tiled=True),
        lax.all_to_all(outgoing(dt_pairs), "grp", split_axis=0, concat_axis=0, tiled=True),
    )
    bc_whole = lax.all_gather(incoming(bc_recv), "ch", axis=2, tiled=True)

    def one_pair(pair_fragments):
        return mix_pair(
            pair_fragments[0],
            pair_fragments[1],
            pair_fragments[2].reshape(pair_len, head_local),
            conv_x,
            conv_x_bias,
            conv_bc,
            conv_bc_bias,
            decay_rate,
            skip_d,
        )

    mixed = lax.map(one_pair, (incoming(x_recv), bc_whole, incoming(dt_recv)))
    mixed = jnp.where(filled[:, None, None], mixed, jnp.zeros_like(mixed))
    returned = lax.all_to_all(
        mixed.reshape(pair_count * pair_len, chan_width),
        "ch",
        split_axis=0,
        concat_axis=1,
        tiled=True,
    )
    values = returned.astype(jnp.float32)
    scale = lax.rsqrt(jnp.mean(values * values, axis=1, keepdims=True) + 1e-05)
    return (values * scale * norm_gain[None, :]).astype(jnp.bfloat16)


def solution(mesh):
    placed = (
        P(("grp", "ch"), None),
        P(("grp", "ch"), None),
        P(("grp", "ch"), None),
        P(),
        P("ch"),
        P("ch"),
        P(None, "ch"),
        P("ch"),
        P(),
        P(),
        P(),
        P(),
        P(),
        P(),
    )
    return jax.shard_map(
        per_device, mesh=mesh, in_specs=placed, out_specs=P(("grp", "ch"), None), check_vma=False
    )
```

profile of v0, /device:TPU:1, one launch (start us, length us, event | category | flops | bytes accessed | tf_op | source)
XLA Modules:
  0.0 517.6 jit_solution(307897756995665700)
XLA Ops:
  10.1 16.7 %all-to-all-start.2 = ((bf16[128,32,8]{0,2,1:T(8,128)(2,1)}), bf16[128,32,8]{0,2,1:T(8,128)(2,1)S(1)}, u32[]{:S(2)}, u32[]{:S(2)}) async-start(bf16[128,32,8]{0,2,1:T(8,128)(2,1)} %select_bitcast_fusion), calls=%async_computation.2 | async-start | bytes 131072 | tf_op jit(solution)/shard_map/all_to_all | solution.py:112
  28.7 3.2 copy.84
  32.8 7.1 %all-to-all-done.2 = bf16[128,32,8]{0,2,1:T(8,128)(2,1)S(1)} async-done(((bf16[128,32,8]{0,2,1:T(8,128)(2,1)}), bf16[128,32,8]{0,2,1:T(8,128)(2,1)S(1)}, u32[]{:S(2)}, u32[]{:S(2)}) %all-to-all-start.2) | async-done | bytes 65568 | tf_op jit(solution)/shard_map/all_to_all | solution.py:112
  39.8 5.1 all-to-all-start.4
  46.3 10.8 %all-to-all-done.4 = bf16[128,32,4]{0,2,1:T(4,128)(2,1)S(1)} async-done(((bf16[128,32,4]{0,2,1:T(4,128)(2,1)}), bf16[128,32,4]{0,2,1:T(4,128)(2,1)S(1)}, u32[]{:S(2)}, u32[]{:S(2)}) %all-to-all-start.4) | async-done | bytes 32800 | tf_op jit(solution)/shard_map/all_to_all | solution.py:113
  57.1 6.8 %all-to-all-start.3 = ((bf16[16,2,256,8]{2,3,1,0:T(8,128)(2,1)}), bf16[16,2,256,8]{2,3,1,0:T(8,128)(2,1)S(1)}, u32[]{:S(2)}, u32[]{:S(2)}) async-start(bf16[16,2,256,8]{2,3,1,0:T(8,128)(2,1)} %broadcast_select_fusion.5), calls=%async_computation.3 | async-start | bytes 262144 | tf_op jit(solution)/shard_map/all_to_all | solution.py:133
  63.8 1.5 broadcast_select_fusion.3
  65.3 5.5 %all-to-all-done.3 = bf16[16,2,256,8]{2,3,1,0:T(8,128)(2,1)S(1)} async-done(((bf16[16,2,256,8]{2,3,1,0:T(8,128)(2,1)}), bf16[16,2,256,8]{2,3,1,0:T(8,128)(2,1)S(1)}, u32[]{:S(2)}, u32[]{:S(2)}) %all-to-all-start.3) | async-done | bytes 131104 | tf_op jit(solution)/shard_map/all_to_all | solution.py:133
  70.8 6.3 %all-to-all-start = ((bf16[128,32,256]{0,2,1:T(8,128)(2,1)}), bf16[128,32,256]{0,2,1:T(8,128)(2,1)S(1)}, u32[]{:S(2)}, u32[]{:S(2)}) async-start(bf16[128,32,256]{0,2,1:T(8,128)(2,1)} %bitcast.147), calls=%async_computation | async-start | bytes 4194304 | tf_op jit(solution)/shard_map/all_to_all | solution.py:111
  78.6 2.0 reshape.292
  82.6 93.4 %all-to-all-done = bf16[128,32,256]{0,2,1:T(8,128)(2,1)S(1)} async-done(((bf16[128,32,256]{0,2,1:T(8,128)(2,1)}), bf16[128,32,256]{0,2,1:T(8,128)(2,1)S(1)}, u32[]{:S(2)}, u32[]{:S(2)}) %all-to-all-start) | async-done | bytes 2097184 | tf_op jit(solution)/shard_map/all_to_all | solution.py:111
  176.0 3.5 all-to-all-start.5
  179.5 3.3 copy.85
  182.7 2.8 gather_fusion.1
  185.5 4.5 broadcast_select_fusion
  190.0 6.8 %all-to-all-start.1 = ((bf16[16,2,256,256]{3,2,1,0:T(8,128)(2,1)}), bf16[16,2,256,256]{3,2,1,0:T(8,128)(2,1)}, u32[]{:S(2)}, u32[]{:S(2)}) async-start(bf16[16,2,256,256]{3,2,1,0:T(8,128)(2,1)} %broadcast_select_fusion), calls=%async_computation.1 | async-start | bytes 8388608 | tf_op jit(solution)/shard_map/all_to_all | solution.py:132
  198.4 53.1 %all-to-all-done.1 = bf16[16,2,256,256]{3,2,1,0:T(8,128)(2,1)} async-done(((bf16[16,2,256,256]{3,2,1,0:T(8,128)(2,1)}), bf16[16,2,256,256]{3,2,1,0:T(8,128)(2,1)}, u32[]{:S(2)}, u32[]{:S(2)}) %all-to-all-start.1) | async-done | bytes 4194336 | tf_op jit(solution)/shard_map/all_to_all | solution.py:132
  251.6 2.9 gather_fusion.2
  254.5 1.6 broadcast_select_fusion.1
  256.1 11.1 %all-gather.2.cloned.1.call-done = bf16[16,256,256]{1,2,0:T(8,128)(2,1)} async-done(((bf16[16,256,8]{1,2,0:T(8,128)(2,1)}), bf16[16,256,256]{1,2,0:T(8,128)(2,1)}) %all-gather.2.cloned.1.call-update) | async-done | bytes 2097168 | tf_op jit(solution)/shard_map/all_gather | solution.py:136
  267.2 119.3 %while.11 = (s32[]{:T(128)}, bf16[16,256,256]{2,1,0:T(8,128)(2,1)}, f32[256]{0:T(256)S(1)}, f32[4,256]{1,0:T(4,128)S(1)}, bf16[16,256,256]{2,1,0:T(8,128)(2,1)},...) while((s32[]{:T(128)}, bf16[16,256,256]{2,1,0:T(8,128)(2,1)}, ...), condition=%wide.region_9.10_spmd.clone, body=%wide.region_6.9_spmd.sunk.clone | while | flops 305400832 | bytes 4293649 | solution.py:151
  272.5 1.4 fusion.74
  280.0 1.4 fusion.74
  302.3 1.4 fusion.74
  317.2 1.4 fusion.74
  332.1 1.4 fusion.74
  386.5 1.8 broadcast_select_fusion.2
  388.3 107.9 %all_to_all.76 = bf16[32,128,256]{2,1,0:T(8,128)(2,1)S(1)} all-to-all(bf16[32,128,256]{2,1,0:T(8,128)(2,1)S(1)} %bitcast.148), channel_id=1, replica_groups=mesh['grp'=16,'ch'=32] {'ch'}, dimensions={0} | all-to-all | bytes 4194304 | tf_op jit(solution)/shard_map/all_to_all | solution.py:153
  496.2 2.4 convert_bitcast_fusion
  498.7 5.6 %copy.92 = f32[128,32,256]{0,2,1:T(8,128)} copy(f32[128,32,256]{2,0,1:T(8,128)} %convert_bitcast_fusion) | data formatting | bytes 8388608 | tf_op jit(solution)/shard_map/convert_element_type | solution.py:160
  505.0 2.8 fusion.34
  507.8 2.9 copy.93
  (466 shorter events, 124.1 us)
Async XLA Ops:
  10.1 29.8 %all-to-all-start.2 = ((bf16[128,32,8]{0,2,1:T(8,128)(2,1)}), bf16[128,32,8]{0,2,1:T(8,128)(2,1)S(1)}, u32[]{:S(2)}, u32[]{:S(2)}) async-start(bf16[128,32,8]{0,2,1:T(8,128)(2,1)} %select_bitcast_fusion), calls=%async_computation.2 | async-start | bytes 131072 | tf_op jit(solution)/shard_map/all_to_all | solution.py:112
  28.6 3.3 copy-start.4
  28.6 3.4 copy-start.9
  39.8 17.3 %all-to-all-start.4 = ((bf16[128,32,4]{0,2,1:T(4,128)(2,1)}), bf16[128,32,4]{0,2,1:T(4,128)(2,1)S(1)}, u32[]{:S(2)}, u32[]{:S(2)}) async-start(bf16[128,32,4]{0,2,1:T(4,128)(2,1)} %bitcast.37), calls=%async_computation.4 | async-start | bytes 65536 | tf_op jit(solution)/shard_map/all_to_all | solution.py:113
  57.1 13.7 %all-to-all-start.3 = ((bf16[16,2,256,8]{2,3,1,0:T(8,128)(2,1)}), bf16[16,2,256,8]{2,3,1,0:T(8,128)(2,1)S(1)}, u32[]{:S(2)}, u32[]{:S(2)}) async-start(bf16[16,2,256,8]{2,3,1,0:T(8,128)(2,1)} %broadcast_select_fusion.5), calls=%async_computation.3 | async-start | bytes 262144 | tf_op jit(solution)/shard_map/all_to_all | solution.py:133
  70.8 6.4 %copy-start.7 = (s32[256]{0:T(256)S(1)}, s32[256]{0:T(256)}, u32[]{:S(2)}) copy-start(s32[256]{0:T(256)} %param.28) | copy-start | bytes 3076
  70.8 6.4 %copy-start.8 = (s32[256]{0:T(256)S(1)}, s32[256]{0:T(256)}, u32[]{:S(2)}) copy-start(s32[256]{0:T(256)} %param.29) | copy-start | bytes 3076
  70.8 105.2 %all-to-all-start = ((bf16[128,32,256]{0,2,1:T(8,128)(2,1)}), bf16[128,32,256]{0,2,1:T(8,128)(2,1)S(1)}, u32[]{:S(2)}, u32[]{:S(2)}) async-start(bf16[128,32,256]{0,2,1:T(8,128)(2,1)} %bitcast.147), calls=%async_computation | async-start | bytes 4194304 | tf_op jit(solution)/shard_map/all_to_all | solution.py:111
  176.0 3.5 copy-start
  176.0 14.0 %all-to-all-start.5 = ((bf16[16,2,1024]{2,1,0:T(2,128)(2,1)}), bf16[16,2,1024]{2,1,0:T(2,128)(2,1)S(1)}, u32[]{:S(2)}, u32[]{:S(2)}) async-start(bf16[16,2,1024]{2,1,0:T(2,128)(2,1)} %broadcast_select_fusion.4), calls=%async_computation.5 | async-start | bytes 131072 | tf_op jit(solution)/shard_map/all_to_all | solution.py:134
  190.0 7.6 %copy-start.10 = (f32[4]{0:T(128)S(1)}, f32[4]{0:T(128)}, u32[]{:S(2)}) copy-start(f32[4]{0:T(128)} %param.20) | copy-start | bytes 52
  190.0 61.6 %all-to-all-start.1 = ((bf16[16,2,256,256]{3,2,1,0:T(8,128)(2,1)}), bf16[16,2,256,256]{3,2,1,0:T(8,128)(2,1)}, u32[]{:S(2)}, u32[]{:S(2)}) async-start(bf16[16,2,256,256]{3,2,1,0:T(8,128)(2,1)} %broadcast_select_fusion), calls=%async_computation.1 | async-start | bytes 8388608 | tf_op jit(solution)/shard_map/all_to_all | solution.py:132
  196.8 70.4 %all-gather.2.cloned.1.call-start = ((), (), s32[]{:S(2)}) async-start(), calls=%async_computation.7 | async-start | bytes 2162688 | tf_op jit(solution)/shard_map/all_gather | solution.py:136
  254.5 12.7 %copy-start.1 = (f32[4,256]{1,0:T(4,128)S(1)}, f32[4,256]{1,0:T(4,128)}, u32[]{:S(2)}) copy-start(f32[4,256]{1,0:T(4,128)} %param.22) | copy-start | bytes 12292
  254.5 12.7 %copy-start.2 = (f32[4,256]{1,0:T(4,128)S(1)}, f32[4,256]{1,0:T(4,128)}, u32[]{:S(2)}) copy-start(f32[4,256]{1,0:T(4,128)} %param.24) | copy-start | bytes 12292
  254.5 12.7 %copy-start.5 = (f32[256]{0:T(256)S(1)}, f32[256]{0:T(256)}, u32[]{:S(2)}) copy-start(f32[256]{0:T(256)} %param.23) | copy-start | bytes 3076
  254.5 12.7 %copy-start.6 = (f32[256]{0:T(256)S(1)}, f32[256]{0:T(256)}, u32[]{:S(2)}) copy-start(f32[256]{0:T(256)} %param.25) | copy-start | bytes 3076
  254.5 12.7 %copy-start.11 = (f32[4]{0:T(128)S(1)}, f32[4]{0:T(128)}, u32[]{:S(2)}) copy-start(f32[4]{0:T(128)} %param.21) | copy-start | bytes 52
  504.2 0.8 copy-start.3
Sparse Core Ops, SparseCore 0:
  199.6 67.5 all-gather.1
where the time goes:
time: 519 us; the launch traced here: 518 us
  waiting for transfers between devices  181 us (35%)
  blocking collectives  108 us (21%)
  other arithmetic  71.4 us (14%)
  local copies, waits for them, and re-layouts  68 us (13%)
  starting transfers between devices  45.2 us (9%)
  matrix products  28.8 us (6%)
  between operations  13.7 us (3%)
    all_to_all x1, blocking collectives, per_device(): lax.all_to_all(mixed.reshape(pair_count * pair_len, chan_width), 'ch', sp...  108 us
    all_to_all x1, waiting for transfers between devices, per_device(): lax.all_to_all(x_masked, 'ch', split_axis=1, concat_axis=0, tiled=True)  93.4 us
    all_to_all x1, waiting for transfers between devices, per_device(): lax.all_to_all(outgoing(x_pairs), 'grp', split_axis=0, concat_axis=0, til...  53.1 us
    dot_general x16, matrix products, mix_pair(): jnp.einsum('hts,shp->thp', weights, x_heads, precision=lax.Precision.HIGH...  22.2 us
    another operation x33, other arithmetic  20 us
    all_to_all x1, starting transfers between devices, per_device(): lax.all_to_all(bc_masked, 'ch', split_axis=1, concat_axis=0, tiled=True)  16.7 us
    dynamic_slice x32, local copies, waits for them, and re-layouts, per_device(): mixed = lax.map(one_pair, (incoming(x_recv), bc_whole, incoming(dt_recv)))  16.2 us
    convert_element_type x16, other arithmetic, mix_pair(): bc_conv = conv_silu(bc_pair.astype(jnp.float32), conv_bc, conv_bc_bias)  14.9 us
  transfers between devices with their start and end apart: 7, of which 6 were waited for; matrix products, arithmetic and copies ran while one was open for 6% of the time, Pallas kernels for 0%

commit v1 on v0

--- a/solution.py
+++ b/solution.py
@@ -133,7 +133,9 @@
         lax.all_to_all(outgoing(bc_col_pairs), "grp", split_axis=0, concat_axis=0, tiled=True),
         lax.all_to_all(outgoing(dt_pairs), "grp", split_axis=0, concat_axis=0, tiled=True),
     )
-    bc_whole = lax.all_gather(incoming(bc_recv), "ch", axis=2, tiled=True)
+    bc_whole = jnp.concatenate(
+        lax.all_to_all(jnp.stack([incoming(bc_recv)] * lax.axis_size("ch")), "ch", 0, 0), axis=2
+    )
 
     def one_pair(pair_fragments):
         return mix_pair(

time: 519 us -> 603 us (1.16)
  waiting for transfers between devices: 181 us -> 268 us
  between operations: 13.7 us -> 0.31 us
    all_to_all x0 -> x1, waiting for transfers between devices: none -> 87.9 us  [per_device(): lax.all_to_all(jnp.stack([incoming(bc_recv)] * lax.axis_size('ch')), 'ch'...]
    all_to_all x1, starting transfers between devices: 16.7 us -> 4.66 us  [per_device(): lax.all_to_all(bc_masked, 'ch', split_axis=1, concat_axis=0, tiled=True)]
    all_to_all x1, starting transfers between devices: 5.12 us -> 16.7 us  [per_device(): lax.all_to_all(step_rows, 'ch', split_axis=1, concat_axis=0, tiled=True)]
    all_gather x1 -> x0, waiting for transfers between devices: 11.1 us -> none  [per_device(): bc_whole = lax.all_gather(incoming(bc_recv), 'ch', axis=2, tiled=True)]
  transfers between devices with their start and end apart: 7 -> 7, of which waited for: 6 -> 7; matrix products, arithmetic and copies ran while one was open for 6% -> 5% of each run, Pallas kernels for 0% -> 0%
where the time goes in v1:
time: 603 us; the launch traced here: 602 us
  waiting for transfers between devices  268 us (44%)
  blocking collectives  107 us (18%)
  local copies, waits for them, and re-layouts  74 us (12%)
  other arithmetic  71.4 us (12%)
  starting transfers between devices  50.8 us (8%)
  matrix products  28.8 us (5%)
    all_to_all x1, blocking collectives, per_device(): lax.all_to_all(mixed.reshape(pair_count * pair_len, chan_width), 'ch', sp...  107 us
    all_to_all x1, waiting for transfers between devices, per_device(): lax.all_to_all(x_masked, 'ch', split_axis=1, concat_axis=0, tiled=True)  96.6 us
    all_to_all x1, waiting for transfers between devices, per_device(): lax.all_to_all(jnp.stack([incoming(bc_recv)] * lax.axis_size('ch')), 'ch'...  87.9 us
    all_to_all x1, waiting for transfers between devices, per_device(): lax.all_to_all(outgoing(x_pairs), 'grp', split_axis=0, concat_axis=0, til...  58.4 us
    dot_general x16, matrix products, mix_pair(): jnp.einsum('hts,shp->thp', weights, x_heads, precision=lax.Precision.HIGH...  22.2 us
    another operation x33, other arithmetic  20 us
    all_to_all x1, starting transfers between devices, per_device(): lax.all_to_all(step_rows, 'ch', split_axis=1, concat_axis=0, tiled=True)  16.7 us
    dynamic_slice x32, local copies, waits for them, and re-layouts, per_device(): mixed = lax.map(one_pair, (incoming(x_recv), bc_whole, incoming(dt_recv)))  16.2 us
  transfers between devices with their start and end apart: 7, of which 7 were waited for; matrix products, arithmetic and copies ran while one was open for 5% of the time, Pallas kernels for 0%

profile of v1, /device:TPU:1, one launch (start us, length us, event | category | flops | bytes accessed | tf_op | source)
XLA Modules:
  0.0 601.6 jit_solution(13695391256754699704)
XLA Ops:
  4.2 16.7 %all-to-all-start.5 = ((bf16[128,32,4]{0,2,1:T(4,128)(2,1)}), bf16[128,32,4]{0,2,1:T(4,128)(2,1)S(1)}, u32[]{:S(2)}, u32[]{:S(2)}) async-start(bf16[128,32,4]{0,2,1:T(4,128)(2,1)} %bitcast.39), calls=%async_computation.5 | async-start | bytes 65536 | tf_op jit(solution)/shard_map/all_to_all | solution.py:113
  24.3 8.6 %all-to-all-done.5 = bf16[128,32,4]{0,2,1:T(4,128)(2,1)S(1)} async-done(((bf16[128,32,4]{0,2,1:T(4,128)(2,1)}), bf16[128,32,4]{0,2,1:T(4,128)(2,1)S(1)}, u32[]{:S(2)}, u32[]{:S(2)}) %all-to-all-start.5) | async-done | bytes 32800 | tf_op jit(solution)/shard_map/all_to_all | solution.py:113
  33.0 4.7 all-to-all-start.2
  37.7 3.2 copy.85
  41.4 2.0 reshape.302
  44.8 5.8 all-to-all-done.2
  50.7 6.8 %all-to-all-start.6 = ((bf16[16,2,1024]{2,1,0:T(2,128)(2,1)}), bf16[16,2,1024]{2,1,0:T(2,128)(2,1)S(1)}, u32[]{:S(2)}, u32[]{:S(2)}) async-start(bf16[16,2,1024]{2,1,0:T(2,128)(2,1)} %broadcast_select_fusion.4), calls=%async_computation.6 | async-start | bytes 131072 | tf_op jit(solution)/shard_map/all_to_all | solution.py:134
  58.8 5.2 all-to-all-done.6
  64.0 3.5 all-to-all-start.3
  67.5 1.5 broadcast_select_fusion.3
  69.0 5.3 all-to-all-done.3
  74.3 9.1 %all-to-all-start = ((bf16[128,32,256]{0,2,1:T(8,128)(2,1)}), bf16[128,32,256]{0,2,1:T(8,128)(2,1)S(1)}, u32[]{:S(2)}, u32[]{:S(2)}) async-start(bf16[128,32,256]{0,2,1:T(8,128)(2,1)} %bitcast.152), calls=%async_computation | async-start | bytes 4194304 | tf_op jit(solution)/shard_map/all_to_all | solution.py:111
  85.1 96.6 %all-to-all-done = bf16[128,32,256]{0,2,1:T(8,128)(2,1)S(1)} async-done(((bf16[128,32,256]{0,2,1:T(8,128)(2,1)}), bf16[128,32,256]{0,2,1:T(8,128)(2,1)S(1)}, u32[]{:S(2)}, u32[]{:S(2)}) %all-to-all-start) | async-done | bytes 2097184 | tf_op jit(solution)/shard_map/all_to_all | solution.py:111
  181.7 1.8 stack.2
  183.7 5.5 all-to-all-start.4
  189.2 3.3 copy.86
  192.5 2.8 gather_fusion.1
  195.3 4.5 broadcast_select_fusion
  199.8 87.9 %all-to-all-done.4 = bf16[32,16,256,8]{2,3,1,0:T(8,128)(2,1)} async-done(((bf16[32,16,256,8]{2,3,1,0:T(8,128)(2,1)}), bf16[32,16,256,8]{2,3,1,0:T(8,128)(2,1)}, u32[]{:S(2)}, u32[]{:S(2)}) %all-to-all-start.4) | async-done | bytes 2097184 | tf_op jit(solution)/shard_map/all_to_all | solution.py:137
  287.6 4.5 all-to-all-start.1
  293.0 3.2 copy.103
  296.2 58.4 %all-to-all-done.1 = bf16[16,2,256,256]{3,2,1,0:T(8,128)(2,1)} async-done(((bf16[16,2,256,256]{3,2,1,0:T(8,128)(2,1)}), bf16[16,2,256,256]{3,2,1,0:T(8,128)(2,1)}, u32[]{:S(2)}, u32[]{:S(2)}) %all-to-all-start.1) | async-done | bytes 4194336 | tf_op jit(solution)/shard_map/all_to_all | solution.py:132
  354.6 2.9 gather_fusion.2
  357.6 1.6 broadcast_select_fusion.1
  359.2 119.3 %while.11 = (s32[]{:T(128)}, bf16[16,256,256]{2,1,0:T(8,128)(2,1)}, f32[256]{0:T(256)S(1)}, f32[4,256]{1,0:T(4,128)S(1)}, bf16[16,256,256]{2,1,0:T(8,128)(2,1)},...) while((s32[]{:T(128)}, bf16[16,256,256]{2,1,0:T(8,128)(2,1)}, ...), condition=%wide.region_9.10_spmd.clone, body=%wide.region_6.9_spmd.sunk.clone | while | flops 305400832 | bytes 4293649 | solution.py:153
  364.5 1.4 fusion.74
  478.5 1.8 broadcast_select_fusion.2
  480.3 106.8 %all_to_all.81 = bf16[32,128,256]{2,1,0:T(8,128)(2,1)S(1)} all-to-all(bf16[32,128,256]{2,1,0:T(8,128)(2,1)S(1)} %bitcast.153), channel_id=1, replica_groups=mesh['grp'=16,'ch'=32] {'ch'}, dimensions={0} | all-to-all | bytes 4194304 | tf_op jit(solution)/shard_map/all_to_all | solution.py:155
  587.1 2.4 convert_bitcast_fusion
  589.5 5.6 copy.94
  595.9 2.8 fusion.34
  598.7 2.9 copy.95
  (463 shorter events, 130.6 us)
Async XLA Ops:
  4.2 28.8 %all-to-all-start.5 = ((bf16[128,32,4]{0,2,1:T(4,128)(2,1)}), bf16[128,32,4]{0,2,1:T(4,128)(2,1)S(1)}, u32[]{:S(2)}, u32[]{:S(2)}) async-start(bf16[128,32,4]{0,2,1:T(4,128)(2,1)} %bitcast.39), calls=%async_computation.5 | async-start | bytes 65536 | tf_op jit(solution)/shard_map/all_to_all | solution.py:113
  33.0 17.7 %all-to-all-start.2 = ((bf16[128,32,8]{0,2,1:T(8,128)(2,1)}), bf16[128,32,8]{0,2,1:T(8,128)(2,1)S(1)}, u32[]{:S(2)}, u32[]{:S(2)}) async-start(bf16[128,32,8]{0,2,1:T(8,128)(2,1)} %select_bitcast_fusion), calls=%async_computation.2 | async-start | bytes 131072 | tf_op jit(solution)/shard_map/all_to_all | solution.py:112
  50.7 13.3 %all-to-all-start.6 = ((bf16[16,2,1024]{2,1,0:T(2,128)(2,1)}), bf16[16,2,1024]{2,1,0:T(2,128)(2,1)S(1)}, u32[]{:S(2)}, u32[]{:S(2)}) async-start(bf16[16,2,1024]{2,1,0:T(2,128)(2,1)} %broadcast_select_fusion.4), calls=%async_computation.6 | async-start | bytes 131072 | tf_op jit(solution)/shard_map/all_to_all | solution.py:134
  64.0 10.3 %all-to-all-start.3 = ((bf16[16,2,256,8]{2,3,1,0:T(8,128)(2,1)}), bf16[16,2,256,8]{2,3,1,0:T(8,128)(2,1)S(1)}, u32[]{:S(2)}, u32[]{:S(2)}) async-start(bf16[16,2,256,8]{2,3,1,0:T(8,128)(2,1)} %broadcast_select_fusion.5), calls=%async_computation.3 | async-start | bytes 262144 | tf_op jit(solution)/shard_map/all_to_all | solution.py:133
  74.3 9.3 %copy-start.6 = (s32[256]{0:T(256)S(1)}, s32[256]{0:T(256)}, u32[]{:S(2)}) copy-start(s32[256]{0:T(256)} %param.28) | copy-start | bytes 3076
  74.3 9.3 %copy-start.7 = (s32[256]{0:T(256)S(1)}, s32[256]{0:T(256)}, u32[]{:S(2)}) copy-start(s32[256]{0:T(256)} %param.29) | copy-start | bytes 3076
  74.3 107.4 %all-to-all-start = ((bf16[128,32,256]{0,2,1:T(8,128)(2,1)}), bf16[128,32,256]{0,2,1:T(8,128)(2,1)S(1)}, u32[]{:S(2)}, u32[]{:S(2)}) async-start(bf16[128,32,256]{0,2,1:T(8,128)(2,1)} %bitcast.152), calls=%async_computation | async-start | bytes 4194304 | tf_op jit(solution)/shard_map/all_to_all | solution.py:111
  181.7 2.0 copy-start
  183.7 103.9 %all-to-all-start.4 = ((bf16[32,16,256,8]{2,3,1,0:T(8,128)(2,1)}), bf16[32,16,256,8]{2,3,1,0:T(8,128)(2,1)}, u32[]{:S(2)}, u32[]{:S(2)}) async-start(bf16[32,16,256,8]{2,3,1,0:T(8,128)(2,1)} %stack.2), calls=%async_computation.4 | async-start | bytes 4194304 | tf_op jit(solution)/shard_map/all_to_all | solution.py:137
  199.8 92.4 %copy-start.8 = (f32[4]{0:T(128)S(1)}, f32[4]{0:T(128)}, u32[]{:S(2)}) copy-start(f32[4]{0:T(128)} %param.20) | copy-start | bytes 52
  287.6 67.0 %all-to-all-start.1 = ((bf16[16,2,256,256]{3,2,1,0:T(8,128)(2,1)}), bf16[16,2,256,256]{3,2,1,0:T(8,128)(2,1)}, u32[]{:S(2)}, u32[]{:S(2)}) async-start(bf16[16,2,256,256]{3,2,1,0:T(8,128)(2,1)} %broadcast_select_fusion), calls=%async_computation.1 | async-start | bytes 8388608 | tf_op jit(solution)/shard_map/all_to_all | solution.py:132
  357.5 1.7 copy-start.1
  357.5 1.7 copy-start.2
  357.5 1.7 copy-start.4
  357.6 1.7 copy-start.5
  357.6 1.6 copy-start.9
  595.1 0.8 copy-start.3
